TPU v7x, 32 devices: a whole 2x2x4 slice. The times are simulated.
32 devices in a mesh: req: 8 (over z, x), grp: 4 (over y, core).
Axes of the slice: x: 2, y: 2, z: 4, core: 2. Of those that a mesh axis runs over, the one named last changes fastest.
Arguments:
- hidden: bfloat16 [256, 16, 1024], P(('grp', 'req')), parts along dimension 0, may hold values from -6 to 6
- norm_gain: float32 [1024], replicated, may hold values from 0.1 to 1.9
- in_weight: bfloat16 [1024, 4096], replicated, may hold values from -0.1875 to 0.1875
- conv_weight: float32 [4, 2048], P(None, 'req'), may hold values from -3 to 3
- conv_bias: float32 [2048], P('req'), may hold values from -3 to 3
- x_weight: bfloat16 [2048, 160], P('req'), may hold values from -0.125 to 0.125
- step_weight: bfloat16 [128, 2048], P(None, 'req'), may hold values from -0.5 to 0.5
- step_bias: float32 [2048], P('req'), may hold values from -5 to -1
- log_decay: float32 [16, 2048], P(None, 'req'), may hold values from -0.7 to 2.8
- skip_gain: float32 [2048], P('req'), may hold values from 0.5 to 1.5
- out_weight: bfloat16 [2048, 1024], replicated, may hold values from -0.125 to 0.125
- old_states: float32 [256, 16, 2048], P(('grp', 'req')), parts along dimension 0, may hold values from -3 to 3
- old_edges: bfloat16 [256, 3, 2048], P(('grp', 'req')), parts along dimension 0, may hold values from -6 to 6
- anchor: int32 [256], P('grp'), parts along dimension 0, may hold values from 0 to 63, each once
- fresh_flag: int32 [256], P('grp'), parts along dimension 0, may hold values 0 or 1
- accepted: int32 [256], P('grp'), parts along dimension 0, may hold values from 1 to 16
- request_ages: int32 [256], P('grp'), parts along dimension 0, may hold values from 0 to 7
Outputs:
- layer_out: bfloat16 [256, 16, 1024], P(('grp', 'req')), parts along dimension 0
- new_states: float32 [256, 16, 2048], P(('grp', 'req')), parts along dimension 0
There are 4 independent parts, one for each index of `grp`. A program takes and returns all parts, laid end to end along the dimension named above; an argument that names none is the same for every part. Nothing has to cross between parts.
Inputs may be any that keep to these rules, and one draw needn't show every extreme that they name: Every old slot is the anchor of exactly one request.
All inputs are finite; a program needn't handle non-finite values.
Results may differ from a plain program's by a relative error of at most 0.0091.
Values may be sent and summed in bfloat16 or wider, within the bound.
No kernel may reach another device: no remote copies, remote signals or barrier semaphores. Data moves between devices by JAX's collectives and lax.ppermute only.
A program may use at most 128 MiB of HBM per device.

v0:
```python
import jax
import jax.numpy as jnp
from jax import lax
from jax.sharding import PartitionSpec as P

EPS = 1e-05


def rms_normed(values_in, norm_gain):
    values = values_in.astype(jnp.float32)
    factor = lax.rsqrt(jnp.mean(values * values, axis=-1, keepdims=True) + EPS)
    return (values * factor * norm_gain).astype(jnp.bfloat16)


def on_device(
    hidden,
    norm_gain,
    in_weight,
    conv_weight,
    conv_bias,
    x_weight,
    step_weight,
    step_bias,
    log_decay,
    skip_gain,
    out_weight,
    old_states,
    old_edges,
    anchor,
    fresh_flag,
    accepted,
    request_ages,
):
    local_reqs, draft_len, width = hidden.shape
    inner_width = out_weight.shape[0]
    channels = conv_weight.shape[1]
    state_size = log_decay.shape[0]
    low_rank = step_weight.shape[0]
    span = old_edges.shape[1]
    state_lead = jnp.swapaxes(old_states, 0, 1)
    edge_lead = jnp.swapaxes(old_edges.astype(jnp.float32), 0, 1)
    moved_states, moved_edges = (
        lax.all_to_all(state_lead, "req", split_axis=2, concat_axis=1, tiled=True),
        lax.all_to_all(edge_lead, "req", split_axis=2, concat_axis=1, tiled=True),
    )
    token_major = jnp.swapaxes(hidden, 0, 1).reshape(draft_len * local_reqs, width)
    normed = rms_normed(token_major, norm_gain)
    projected = jnp.dot(normed, in_weight, preferred_element_type=jnp.float32).astype(jnp.bfloat16)
    projected = jnp.moveaxis(projected.reshape(draft_len, local_reqs, 2, inner_width), 2, 0)
    grouped = lax.all_to_all(projected, "req", split_axis=3, concat_axis=2, tiled=True)
    all_reqs = grouped.shape[2]
    inner_part = grouped[0]
    gate_part = grouped[1]
    keep_state = (1 - fresh_flag).astype(jnp.float32)
    start_state = jnp.take(moved_states, anchor, axis=1) * keep_state[None, :, None]
    edges = jnp.take(moved_edges, anchor, axis=1)
    distance = span - jnp.arange(span, dtype=jnp.int32)
    usable = (distance[:, None] <= request_ages[None, :]) & (fresh_flag[None, :] == 0)
    history = jnp.where(usable[:, :, None], edges, jnp.zeros((), jnp.float32))
    sequence = jnp.concatenate([history, inner_part.astype(jnp.float32)], axis=0)
    running = conv_bias + conv_weight[0] * sequence[0:draft_len]
    for offset in range(1, conv_weight.shape[0]):
        running = running + conv_weight[offset] * sequence[offset : offset + draft_len]
    conv_out = jax.nn.silu(running).astype(jnp.bfloat16)
    conv_rows = conv_out.reshape(draft_len * all_reqs, channels)
    partial_value = jnp.dot(conv_rows, x_weight, preferred_element_type=jnp.float32)
    mixed_rows = lax.psum(partial_value, "req").astype(jnp.bfloat16)
    flat = all_reqs * channels
    step_sizes = jax.nn.softplus(
        jnp.dot(mixed_rows[:, :low_rank], step_weight, preferred_element_type=jnp.float32)
        + step_bias
    )
    step_sizes = step_sizes.reshape(draft_len, flat)
    coeffs = (
        mixed_rows[:, low_rank:].astype(jnp.float32).reshape(draft_len, all_reqs, 2 * state_size)
    )
    b_coeff = coeffs[:, :, :state_size]
    c_coeff = coeffs[:, :, state_size:]
    inputs = conv_out.astype(jnp.float32)
    flat_inputs = inputs.reshape(draft_len, flat)
    decay = jnp.broadcast_to(
        (-jnp.exp(log_decay))[:, None, :], (state_size, all_reqs, channels)
    ).reshape(state_size, flat)
    start_flat = start_state.reshape(state_size, flat)

    def spread(per_token):
        return jnp.broadcast_to(
            jnp.swapaxes(per_token, 0, 1)[:, :, None], (state_size, all_reqs, channels)
        ).reshape(state_size, flat)

    def advance(carried, sliced):
        current, chosen = carried
        step_delta, step_b, step_c, step_input, step_index = sliced
        factor = jnp.exp(step_delta[None, :] * decay)
        current = factor * current + (step_delta * step_input)[None, :] * spread(step_b)
        result = jnp.sum(spread(step_c) * current, axis=0)
        picked = jnp.broadcast_to(
            (accepted == step_index + 1)[:, None], (all_reqs, channels)
        ).reshape(flat)
        chosen = jnp.where(picked[None, :], current, chosen)
        return ((current, chosen), result)

    sliced = (step_sizes, b_coeff, c_coeff, flat_inputs, jnp.arange(draft_len, dtype=jnp.int32))
    (final_state, chosen), outputs = lax.scan(advance, (start_flat, start_flat), sliced)
    outputs = outputs.reshape(draft_len, all_reqs, channels)
    gated_rows = (
        (outputs + skip_gain * inputs) * jax.nn.silu(gate_part.astype(jnp.float32))
    ).astype(jnp.bfloat16)
    returned = lax.all_to_all(gated_rows, "req", split_axis=1, concat_axis=2, tiled=True)
    layer_out = jnp.dot(
        returned.reshape(draft_len * local_reqs, inner_width),
        out_weight,
        preferred_element_type=jnp.float32,
    ).astype(jnp.bfloat16)
    layer_out = jnp.swapaxes(layer_out.reshape(draft_len, local_reqs, width), 0, 1)
    owned = lax.all_to_all(
        chosen.reshape(state_size, all_reqs, channels),
        "req",
        split_axis=1,
        concat_axis=2,
        tiled=True,
    )
    return (layer_out, jnp.swapaxes(owned, 0, 1))


def solution(mesh):
    return jax.shard_map(
        on_device,
        mesh=mesh,
        in_specs=(
            P(("grp", "req"), None, None),
            P(),
            P(),
            P(None, "req"),
            P("req"),
            P("req", None),
            P(None, "req"),
            P("req"),
            P(None, "req"),
            P("req"),
            P(),
            P(("grp", "req"), None, None),
            P(("grp", "req"), None, None),
            P("grp"),
            P("grp"),
            P("grp"),
            P("grp"),
        ),
        out_specs=(P(("grp", "req"), None, None), P(("grp", "req"), None, None)),
        check_vma=False,
    )
```

profile of v0, /device:TPU:0, one launch (start us, length us, event | category | flops | bytes accessed | tf_op | source)
XLA Modules:
  0.0 369.8 jit_solution(14479661632174473123)
XLA Ops:
  0.7 4.0 %copy.100 = f32[8,3,2048]{0,1,2:T(4,128)} copy(bf16[8,3,2048]{2,0,1:T(8,128)(2,1)} %param.31) | data formatting | bytes 294912 | tf_op jit(solution)/shard_map/transpose | solution.py:41
  4.7 3.9 %bitcast_bitcast_fusion.2 = f32[2048,3,8]{2,1,0:T(4,128)} fusion(f32[8,3,2048]{0,1,2:T(4,128)} %copy.100), kind=kLoop, calls=%fused_computation.72 | loop fusion | bytes 393216
  8.6 5.1 %reshape.188 = f32[8,1,6144]{2,1,0:T(1,128)} reshape(f32[2048,3,8]{2,1,0:T(4,128)} %bitcast_bitcast_fusion.2) | data formatting | bytes 393216
  13.7 7.3 %all-to-all-start.1 = ((f32[8,1,6144]{2,1,0:T(1,128)}), f32[8,1,6144]{2,1,0:T(1,128)S(1)}, u32[]{:S(2)}, u32[]{:S(2)}) async-start(f32[8,1,6144]{2,1,0:T(1,128)} %reshape.188), calls=%async_computation.1 | async-start | bytes 393216 | tf_op jit(solution)/shard_map/all_to_all | solution.py:44
  20.9 4.7 %copy.94 = f32[8,16,2048]{1,0,2:T(8,128)} copy(f32[8,16,2048]{2,1,0:T(8,128)S(1)} %copy-done.3) | data formatting | bytes 2097152 | tf_op args[11]
  26.0 4.8 %convolution_convert_fusion = bf16[128,4096]{1,0:T(8,128)(2,1)S(1)} fusion(bf16[1024,4096]{1,0:T(8,128)(2,1)} %param.21, f32[1024]{0:T(1024)S(1)} %copy-done.4, f32[128]{0:T(128)S(1)} %rsqrt.12, bf16[8,16,1024]{2,1,0:T(8,128)(2,1)S(1)} %copy-done.2), kind=kOutput, calls=%fused_computation.11 | convolution fusion | flops 1074790400 | bytes 9703936 | tf_op jit(solution)/shard_map/dot_general | solution.py:48
  30.8 8.9 %copy.103 = bf16[16,8,2,2048]{0,1,2,3:T(8,128)(2,1)} copy(bf16[16,8,2,2048]{3,1,2,0:T(8,128)(2,1)S(1)} %bitcast.169) | data formatting | bytes 2097152 | tf_op jit(solution)/shard_map/reshape | solution.py:49
  39.6 7.5 %bitcast_bitcast_fusion = bf16[2048,2,8,16]{3,2,1,0:T(8,128)(2,1)} fusion(bf16[16,8,2,2048]{0,1,2,3:T(8,128)(2,1)} %copy.103), kind=kLoop, calls=%fused_computation.70 | loop fusion | bytes 2097152
  47.1 5.8 %bitcast_bitcast_fusion.1 = f32[2048,8,16]{2,1,0:T(8,128)} fusion(f32[8,16,2048]{1,0,2:T(8,128)} %copy.94), kind=kLoop, calls=%fused_computation.71 | loop fusion | bytes 2097152
  52.9 8.1 %reshape.184 = f32[8,1,32768]{2,1,0:T(1,128)} reshape(f32[2048,8,16]{2,1,0:T(8,128)} %bitcast_bitcast_fusion.1) | data formatting | bytes 2097152
  61.1 6.0 %all-to-all-start = ((f32[8,1,32768]{2,1,0:T(1,128)}), f32[8,1,32768]{2,1,0:T(1,128)S(1)}, u32[]{:S(2)}, u32[]{:S(2)}) async-start(f32[8,1,32768]{2,1,0:T(1,128)} %reshape.184), calls=%async_computation | async-start | bytes 2097152 | tf_op jit(solution)/shard_map/all_to_all | solution.py:43
  67.3 11.3 %reshape.186 = bf16[8,2,32768]{2,1,0:T(2,128)(2,1)} reshape(bf16[2048,2,8,16]{3,2,1,0:T(8,128)(2,1)} %bitcast_bitcast_fusion) | data formatting | bytes 2097152
  80.5 4.7 %reshape.189 = f32[2048,3,8]{2,1,0:T(4,128)} reshape(f32[8,6144]{1,0:T(8,128)S(1)} %reduce.3) | data formatting | bytes 393216
  85.2 3.5 copy.101
  89.6 2.9 all-to-all-done
  92.5 3.7 %all-to-all-start.2 = ((bf16[8,2,32768]{2,1,0:T(2,128)(2,1)}), bf16[8,2,32768]{2,1,0:T(2,128)(2,1)S(1)}, u32[]{:S(2)}, u32[]{:S(2)}) async-start(bf16[8,2,32768]{2,1,0:T(2,128)(2,1)} %reshape.186), calls=%async_computation.2 | async-start | bytes 2097152 | tf_op jit(solution)/shard_map/all_to_all | solution.py:50
  96.3 3.1 reduce.2
  99.4 6.1 %reshape.185 = f32[2048,8,16]{2,1,0:T(8,128)} reshape(f32[8,32768]{1,0:T(8,128)S(1)} %reduce.2) | data formatting | bytes 2097152
  105.5 5.4 %copy.96 = f32[16,8,8,256]{3,2,1,0:T(8,128)S(1)} copy(f32[16,8,8,256]{0,2,3,1:T(8,128)} %bitcast.155) | data formatting | bytes 2097152 | tf_op jit(solution)/shard_map/all_to_all | solution.py:43
  112.4 9.5 %all-to-all-done.2 = bf16[8,2,32768]{2,1,0:T(2,128)(2,1)S(1)} async-done(((bf16[8,2,32768]{2,1,0:T(2,128)(2,1)}), bf16[8,2,32768]{2,1,0:T(2,128)(2,1)S(1)}, u32[]{:S(2)}, u32[]{:S(2)}) %all-to-all-start.2) | async-done | bytes 1048608 | tf_op jit(solution)/shard_map/all_to_all | solution.py:50
  121.9 7.6 %reshape.187 = bf16[2048,2,8,16]{3,2,1,0:T(8,128)(2,1)} reshape(bf16[8,2,32768]{2,1,0:T(2,128)(2,1)S(1)} %all-to-all-done.2) | data formatting | bytes 2097152
  129.5 8.9 %copy.104 = bf16[2,16,8,8,256]{4,2,3,1,0:T(8,128)(2,1)S(1)} copy(bf16[2,16,8,8,256]{1,2,0,4,3:T(8,128)(2,1)} %bitcast.156) | data formatting | bytes 2097152 | tf_op jit(solution)/shard_map/all_to_all | solution.py:50
  140.2 43.6 %all-reduce.1 = bf16[1024,160]{0,1:T(8,128)(2,1)} all-reduce(f32[1024,160]{0,1:T(8,128)S(1)} %fusion.29), channel_id=1, replica_groups=mesh['req'=8,'grp'=4] {'req'}, use_global_device_ids=true, to_apply=%region_1.2 | all-reduce | flops 163840 | bytes 983040 | tf_op jit(solution)/shard_map/psum | solution.py:67
  184.7 2.7 compare_select_fusion
  187.4 2.4 reshape.145
  191.2 132.7 %while.15 = (s32[]{:T(128)}, f32[16,16384]{1,0:T(8,128)S(1)}, f32[16,16384]{1,0:T(8,128)S(1)}, f32[16,16384]{1,0:T(8,128)}, f32[16,16384]{1,0:T(8,128)}, /*index...) while((s32[]{:T(128)}, f32[16,16384]{1,0:T(8,128)S(1)}, ...), condition=%wide.region_4.5_spmd.clone, body=%wide.region_2.4_spmd.clone.sunk | while | flops 1835075 | bytes 18522676 | solution.py:104
  192.9 1.3 constant_dynamic-slice_fusion.6
  197.6 1.9 dynamic_update_slice.6
  201.2 1.3 constant_dynamic-slice_fusion.6
  205.9 1.9 dynamic_update_slice.6
  209.5 1.3 constant_dynamic-slice_fusion.6
  214.2 1.9 dynamic_update_slice.6
  217.8 1.3 constant_dynamic-slice_fusion.6
  222.5 1.9 dynamic_update_slice.6
  226.1 1.3 constant_dynamic-slice_fusion.6
  230.7 1.9 dynamic_update_slice.6
  234.3 1.3 constant_dynamic-slice_fusion.6
  239.0 1.9 dynamic_update_slice.6
  242.6 1.3 constant_dynamic-slice_fusion.6
  247.3 1.9 dynamic_update_slice.6
  250.9 1.3 constant_dynamic-slice_fusion.6
  255.6 1.9 dynamic_update_slice.6
  259.2 1.3 constant_dynamic-slice_fusion.6
  263.9 1.9 dynamic_update_slice.6
  267.5 1.3 constant_dynamic-slice_fusion.6
  272.2 1.9 dynamic_update_slice.6
  275.8 1.3 constant_dynamic-slice_fusion.6
  280.5 1.9 dynamic_update_slice.6
  288.8 1.9 dynamic_update_slice.6
  292.4 1.3 constant_dynamic-slice_fusion.6
  297.1 1.9 dynamic_update_slice.6
  300.7 1.3 constant_dynamic-slice_fusion.6
  305.4 1.9 dynamic_update_slice.6
  313.7 1.9 dynamic_update_slice.6
  317.3 1.3 constant_dynamic-slice_fusion.6
  322.0 1.9 dynamic_update_slice.6
  323.9 1.5 copy.127
  325.5 1.5 fusion.16
  328.1 3.5 all-to-all-start.3
  332.7 9.4 %all-to-all-done.3 = bf16[16,64,256]{2,0,1:T(8,128)(2,1)S(1)} async-done(((bf16[16,64,256]{2,0,1:T(8,128)(2,1)}), bf16[16,64,256]{2,0,1:T(8,128)(2,1)S(1)}, u32[]{:S(2)}, u32[]{:S(2)}) %all-to-all-start.3) | async-done | bytes 524320 | tf_op jit(solution)/shard_map/all_to_all | solution.py:109
  342.1 9.1 %all-to-all-start.4 = ((f32[16,64,256]{2,0,1:T(8,128)}), f32[16,64,256]{2,0,1:T(8,128)S(1)}, u32[]{:S(2)}, u32[]{:S(2)}) async-start(f32[16,64,256]{2,0,1:T(8,128)} %bitcast.121), calls=%async_computation.4 | async-start | bytes 2097152 | tf_op jit(solution)/shard_map/all_to_all | solution.py:116
  351.6 2.9 fusion.2
  355.4 12.2 %all-to-all-done.4 = f32[16,64,256]{2,0,1:T(8,128)S(1)} async-done(((f32[16,64,256]{2,0,1:T(8,128)}), f32[16,64,256]{2,0,1:T(8,128)S(1)}, u32[]{:S(2)}, u32[]{:S(2)}) %all-to-all-start.4) | async-done | bytes 1048608 | tf_op jit(solution)/shard_map/all_to_all | solution.py:116
  368.2 1.6 copy.113
  (283 shorter events, 84.1 us)
Async XLA Ops:
  0.6 139.3 %copy-start = (bf16[256,160]{0,1:T(8,128)(2,1)S(1)}, bf16[256,160]{0,1:T(8,128)(2,1)}, u32[]{:S(2)}) copy-start(bf16[256,160]{0,1:T(8,128)(2,1)} %param.24) | copy-start | bytes 245764
  0.6 20.3 %copy-start.3 = (f32[8,16,2048]{2,1,0:T(8,128)S(1)}, f32[8,16,2048]{2,1,0:T(8,128)}, u32[]{:S(2)}) copy-start(f32[8,16,2048]{2,1,0:T(8,128)} %param.30) | copy-start | bytes 3145732
  8.6 17.1 %copy-start.2 = (bf16[8,16,1024]{2,1,0:T(8,128)(2,1)S(1)}, bf16[8,16,1024]{2,1,0:T(8,128)(2,1)}, u32[]{:S(2)}) copy-start(bf16[8,16,1024]{2,1,0:T(8,128)(2,1)} %param.19) | copy-start | bytes 786436
  8.6 17.4 %copy-start.4 = (f32[1024]{0:T(1024)S(1)}, f32[1024]{0:T(1024)}, u32[]{:S(2)}) copy-start(f32[1024]{0:T(1024)} %param.20) | copy-start | bytes 12292
  13.7 47.4 %all-to-all-start.1 = ((f32[8,1,6144]{2,1,0:T(1,128)}), f32[8,1,6144]{2,1,0:T(1,128)S(1)}, u32[]{:S(2)}, u32[]{:S(2)}) async-start(f32[8,1,6144]{2,1,0:T(1,128)} %reshape.188), calls=%async_computation.1 | async-start | bytes 393216 | tf_op jit(solution)/shard_map/all_to_all | solution.py:44
  52.9 8.2 %copy-start.12 = (s32[64]{0:T(128)S(1)}, s32[64]{0:T(128)}, u32[]{:S(2)}) copy-start(s32[64]{0:T(128)} %param.33) | copy-start | bytes 772
  52.9 14.3 %copy-start.13 = (s32[64]{0:T(128)S(1)}, s32[64]{0:T(128)}, u32[]{:S(2)}) copy-start(s32[64]{0:T(128)} %param.32) | copy-start | bytes 772
  52.9 25.7 %copy-start.9 = (s32[64]{0:T(128)S(1)}, s32[64]{0:T(128)}, u32[]{:S(2)}) copy-start(s32[64]{0:T(128)} %param.35) | copy-start | bytes 772
  52.9 25.9 %copy-start.6 = (f32[4,256]{1,0:T(4,128)S(1)}, f32[4,256]{1,0:T(4,128)}, u32[]{:S(2)}) copy-start(f32[4,256]{1,0:T(4,128)} %param.22) | copy-start | bytes 12292
  52.9 25.9 %copy-start.5 = (f32[16,256]{1,0:T(8,128)S(1)}, f32[16,256]{1,0:T(8,128)}, u32[]{:S(2)}) copy-start(f32[16,256]{1,0:T(8,128)} %param.27) | copy-start | bytes 49156
  61.1 31.4 %all-to-all-start = ((f32[8,1,32768]{2,1,0:T(1,128)}), f32[8,1,32768]{2,1,0:T(1,128)S(1)}, u32[]{:S(2)}, u32[]{:S(2)}) async-start(f32[8,1,32768]{2,1,0:T(1,128)} %reshape.184), calls=%async_computation | async-start | bytes 2097152 | tf_op jit(solution)/shard_map/all_to_all | solution.py:43
  92.5 29.4 %all-to-all-start.2 = ((bf16[8,2,32768]{2,1,0:T(2,128)(2,1)}), bf16[8,2,32768]{2,1,0:T(2,128)(2,1)S(1)}, u32[]{:S(2)}, u32[]{:S(2)}) async-start(bf16[8,2,32768]{2,1,0:T(2,128)(2,1)} %reshape.186), calls=%async_computation.2 | async-start | bytes 2097152 | tf_op jit(solution)/shard_map/all_to_all | solution.py:50
  112.4 27.0 %copy-start.7 = (f32[256]{0:T(256)S(1)}, f32[256]{0:T(256)}, u32[]{:S(2)}) copy-start(f32[256]{0:T(256)} %param.23) | copy-start | bytes 3076
  129.5 55.2 %copy-start.10 = (bf16[128,256]{1,0:T(8,128)(2,1)S(1)}, bf16[128,256]{1,0:T(8,128)(2,1)}, u32[]{:S(2)}) copy-start(bf16[128,256]{1,0:T(8,128)(2,1)} %param.25) | copy-start | bytes 196612
  129.5 55.2 %copy-start.11 = (f32[256]{0:T(256)S(1)}, f32[256]{0:T(256)}, u32[]{:S(2)}) copy-start(f32[256]{0:T(256)} %param.26) | copy-start | bytes 3076
  138.4 1.0 copy-start.1
  138.4 52.8 %copy-start.14 = (s32[64]{0:T(128)S(1)}, s32[64]{0:T(128)}, u32[]{:S(2)}) copy-start(s32[64]{0:T(128)} %param.34) | copy-start | bytes 772
  191.2 134.3 %copy-start.8 = (f32[256]{0:T(256)S(1)}, f32[256]{0:T(256)}, u32[]{:S(2)}) copy-start(f32[256]{0:T(256)} %param.28) | copy-start | bytes 3076
  328.1 14.0 %all-to-all-start.3 = ((bf16[16,64,256]{2,0,1:T(8,128)(2,1)}), bf16[16,64,256]{2,0,1:T(8,128)(2,1)S(1)}, u32[]{:S(2)}, u32[]{:S(2)}) async-start(bf16[16,64,256]{2,0,1:T(8,128)(2,1)} %copy.108), calls=%async_computation.3 | async-start | bytes 1048576 | tf_op jit(solution)/shard_map/all_to_all | solution.py:109
  342.1 25.5 %all-to-all-start.4 = ((f32[16,64,256]{2,0,1:T(8,128)}), f32[16,64,256]{2,0,1:T(8,128)S(1)}, u32[]{:S(2)}, u32[]{:S(2)}) async-start(f32[16,64,256]{2,0,1:T(8,128)} %bitcast.121), calls=%async_computation.4 | async-start | bytes 2097152 | tf_op jit(solution)/shard_map/all_to_all | solution.py:116
where the time goes:
time: 372 us; the launch traced here: 370 us
  local copies, waits for them, and re-layouts  191 us (51%)
  other arithmetic  47.8 us (13%)
  blocking collectives  43.6 us (12%)
  waiting for transfers between devices  33.9 us (9%)
  starting transfers between devices  29.5 us (8%)
  loops' own time  12.3 us (3%)
  matrix products  10.8 us (3%)
    unnamed x47, local copies, waits for them, and re-layouts  70.4 us
    psum x1, blocking collectives, on_device(): mixed_rows = lax.psum(partial_value, 'req').astype(jnp.bfloat16)  43.6 us
    dynamic_update_slice x16, local copies, waits for them, and re-layouts, on_device(): lax.scan(advance, (start_flat, start_flat), sliced)  31.1 us
    while x48, local copies, waits for them, and re-layouts  29.4 us
    dynamic_slice x16, other arithmetic, on_device(): lax.scan(advance, (start_flat, start_flat), sliced)  20.9 us
    reduce_sum x16, other arithmetic, advance(): result = jnp.sum(spread(step_c) * current, axis=0)  14.9 us
    another operation x1, loops' own time, on_device(): lax.scan(advance, (start_flat, start_flat), sliced)  12.3 us
    all_to_all x1, waiting for transfers between devices, on_device(): lax.all_to_all(chosen.reshape(state_size, all_reqs, channels), 'req', spl...  12.2 us
  transfers between devices with their start and end apart: 5, of which 4 were waited for; matrix products, arithmetic and copies ran while one was open for 23% of the time, Pallas kernels for 0%

commit v1 on v0

--- a/solution.py
+++ b/solution.py
@@ -47,7 +47,18 @@
     normed = rms_normed(token_major, norm_gain)
     projected = jnp.dot(normed, in_weight, preferred_element_type=jnp.float32).astype(jnp.bfloat16)
     projected = jnp.moveaxis(projected.reshape(draft_len, local_reqs, 2, inner_width), 2, 0)
-    grouped = lax.all_to_all(projected, "req", split_axis=3, concat_axis=2, tiled=True)
+    ways, here = (lax.axis_size("req"), lax.axis_index("req"))
+    width_2 = projected.shape[3] // ways
+    shape = list(projected.shape)
+    shape[3] = width_2
+    height = shape[2]
+    shape[2] = height * ways
+    grouped = jnp.zeros(shape, projected.dtype)
+    for mask in range(ways):
+        part = lax.dynamic_slice_in_dim(projected, (here ^ mask) * width_2, width_2, axis=3)
+        if mask:
+            part = lax.ppermute(part, "req", [(d, d ^ mask) for d in range(ways)])
+        grouped = lax.dynamic_update_slice_in_dim(grouped, part, (here ^ mask) * height, axis=2)
     all_reqs = grouped.shape[2]
     inner_part = grouped[0]
     gate_part = grouped[1]

time: 372 us -> 330 us (0.89)
  local copies, waits for them, and re-layouts: 191 us -> 142 us
  starting transfers between devices: 29.5 us -> 36.9 us
  waiting for transfers between devices: 33.9 us -> 29.8 us
  other arithmetic: 47.8 us -> 51.6 us
    unnamed x47 -> x51, local copies, waits for them, and re-layouts: 70.4 us -> 43.1 us
    ppermute x0 -> x7, starting transfers between devices: none -> 14.5 us  [on_device(): part = lax.ppermute(part, 'req', [(d, d ^ mask) for d in range(ways)])]
    all_to_all x1 -> x0, waiting for transfers between devices: 9.5 us -> none  [on_device(): lax.all_to_all(projected, 'req', split_axis=3, concat_axis=2, tiled=True)]
    all_to_all x1 -> x0, local copies, waits for them, and re-layouts: 8.9 us -> none  [on_device(): lax.all_to_all(projected, 'req', split_axis=3, concat_axis=2, tiled=True)]
    reshape x1 -> x0, local copies, waits for them, and re-layouts: 8.85 us -> none  [on_device(): projected.reshape(draft_len, local_reqs, 2, inner_width)]
    ppermute x0 -> x7, waiting for transfers between devices: none -> 6.18 us  [on_device(): part = lax.ppermute(part, 'req', [(d, d ^ mask) for d in range(ways)])]
    all_to_all x1 -> x0, starting transfers between devices: 3.74 us -> none  [on_device(): lax.all_to_all(projected, 'req', split_axis=3, concat_axis=2, tiled=True)]
  transfers between devices with their start and end apart: 5 -> 11, of which waited for: 4 -> 4; matrix products, arithmetic and copies ran while one was open for 23% -> 17% of each run, Pallas kernels for 0% -> 0%
where the time goes in v1:
time: 330 us; the launch traced here: 328 us
  local copies, waits for them, and re-layouts  142 us (43%)
  other arithmetic  51.6 us (16%)
  blocking collectives  45.6 us (14%)
  starting transfers between devices  36.9 us (11%)
  waiting for transfers between devices  29.8 us (9%)
  loops' own time  11.8 us (4%)
  matrix products  9.01 us (3%)
    psum x1, blocking collectives, on_device(): mixed_rows = lax.psum(partial_value, 'req').astype(jnp.bfloat16)  45.6 us
    unnamed x51, local copies, waits for them, and re-layouts  43.1 us
    dynamic_update_slice x16, local copies, waits for them, and re-layouts, on_device(): lax.scan(advance, (start_flat, start_flat), sliced)  31 us
    while x48, local copies, waits for them, and re-layouts  29.4 us
    dynamic_slice x16, other arithmetic, on_device(): lax.scan(advance, (start_flat, start_flat), sliced)  20.9 us
    reduce_sum x16, other arithmetic, advance(): result = jnp.sum(spread(step_c) * current, axis=0)  14.9 us
    ppermute x7, starting transfers between devices, on_device(): part = lax.ppermute(part, 'req', [(d, d ^ mask) for d in range(ways)])  14.5 us
    all_to_all x1, waiting for transfers between devices, on_device(): lax.all_to_all(chosen.reshape(state_size, all_reqs, channels), 'req', spl...  12.1 us
  transfers between devices with their start and end apart: 11, of which 4 were waited for; matrix products, arithmetic and copies ran while one was open for 17% of the time, Pallas kernels for 0%

profile of v1, /device:TPU:0, one launch (start us, length us, event | category | flops | bytes accessed | tf_op | source)
XLA Modules:
  0.0 328.4 jit_solution(14531337665926386724)
XLA Ops:
  2.0 4.9 %convolution_convert_fusion = bf16[128,4096]{1,0:T(8,128)(2,1)S(1)} fusion(bf16[1024,4096]{1,0:T(8,128)(2,1)} %param.21, f32[1024]{0:T(1024)} %param.20, f32[128]{0:T(128)S(1)} %rsqrt.12, bf16[8,16,1024]{2,1,0:T(8,128)(2,1)} %param.19), kind=kOutput, calls=%fused_computation.11 | convolution fusion | flops 1074790400 | bytes 9703936 | tf_op jit(solution)/shard_map/dot_general | solution.py:48
  7.1 3.0 collective-permute-start
  10.2 1.6 collective-permute-start.1
  11.9 3.1 collective-permute-start.3
  15.0 1.3 collective-permute-start.4
  16.3 2.7 copy.116
  19.1 3.9 %bitcast_bitcast_fusion.1 = f32[2048,3,8]{2,1,0:T(4,128)} fusion(f32[8,3,2048]{0,1,2:T(4,128)} %copy.116), kind=kLoop, calls=%fused_computation.95 | loop fusion | bytes 393216
  22.9 5.2 %reshape.182 = f32[8,1,6144]{2,1,0:T(1,128)} reshape(f32[2048,3,8]{2,1,0:T(4,128)} %bitcast_bitcast_fusion.1) | data formatting | bytes 393216
  28.1 4.9 %all-to-all-start.1 = ((f32[8,1,6144]{2,1,0:T(1,128)}), f32[8,1,6144]{2,1,0:T(1,128)S(1)}, u32[]{:S(2)}, u32[]{:S(2)}) async-start(f32[8,1,6144]{2,1,0:T(1,128)} %reshape.182), calls=%async_computation.1 | async-start | bytes 393216 | tf_op jit(solution)/shard_map/all_to_all | solution.py:44
  33.0 4.6 %copy.110 = f32[8,16,2048]{1,0,2:T(8,128)} copy(f32[8,16,2048]{2,1,0:T(8,128)S(1)} %copy-done.3) | data formatting | bytes 2097152 | tf_op args[11]
  37.7 5.8 %bitcast_bitcast_fusion = f32[2048,8,16]{2,1,0:T(8,128)} fusion(f32[8,16,2048]{1,0,2:T(8,128)} %copy.110), kind=kLoop, calls=%fused_computation.94 | loop fusion | bytes 2097152
  43.9 8.1 %reshape.180 = f32[8,1,32768]{2,1,0:T(1,128)} reshape(f32[2048,8,16]{2,1,0:T(8,128)} %bitcast_bitcast_fusion) | data formatting | bytes 2097152
  52.3 3.9 %collective-permute-start.5 = (bf16[2,16,8,256]{3,2,1,0:T(8,128)(2,1)S(1)}, bf16[2,16,8,256]{3,2,1,0:T(8,128)(2,1)S(1)}, u32[]{:S(2)}, u32[]{:S(2)}) collective-permute-start(bf16[2,16,8,256]{3,2,1,0:T(8,128)(2,1)S(1)} %bitcast.201), channel_id=1, source_target_pairs={{0,24},{4,28},{8,16},{12,20},{16,8},{20,12},{24,0},{28,4},{1,25},{... | collective-permute-start | bytes 393224 | tf_op jit(solution)/shard_map/ppermute | solution.py:60
  56.2 1.5 collective-permute-start.6
  57.9 1.4 collective-permute-done.5
  59.3 4.8 %collective-permute-done.6 = bf16[2,16,8,256]{3,2,1,0:T(8,128)(2,1)S(1)} collective-permute-done((bf16[2,16,8,256]{3,2,1,0:T(8,128)(2,1)S(1)}, bf16[2,16,8,256]{3,2,1,0:T(8,128)(2,1)S(1)}, u32[]{:S(2)}, u32[]{:S(2)}) %collective-permute-start.6) | collective-permute-done | bytes 131104 | tf_op jit(solution)/shard_map/ppermute | solution.py:60
  65.3 5.1 %all-to-all-start = ((f32[8,1,32768]{2,1,0:T(1,128)}), f32[8,1,32768]{2,1,0:T(1,128)S(1)}, u32[]{:S(2)}, u32[]{:S(2)}) async-start(f32[8,1,32768]{2,1,0:T(1,128)} %reshape.180), calls=%async_computation | async-start | bytes 2097152 | tf_op jit(solution)/shard_map/all_to_all | solution.py:43
  72.1 4.7 %reshape.183 = f32[2048,3,8]{2,1,0:T(4,128)} reshape(f32[8,6144]{1,0:T(8,128)S(1)} %reduce.3) | data formatting | bytes 393216
  76.8 3.5 %copy.117 = f32[3,8,8,256]{3,0,1,2:T(4,128)S(1)} copy(f32[3,8,8,256]{1,0,3,2:T(4,128)} %bitcast.174) | data formatting | bytes 393216 | tf_op jit(solution)/shard_map/all_to_all | solution.py:44
  81.3 3.0 multiply_convert_fusion
  84.6 45.6 %all-reduce.1 = bf16[1024,160]{0,1:T(8,128)(2,1)S(1)} all-reduce(f32[1024,160]{0,1:T(8,128)S(1)} %fusion.30), channel_id=1, replica_groups=mesh['req'=8,'grp'=4] {'req'}, use_global_device_ids=true, to_apply=%region_1.2 | all-reduce | flops 163840 | bytes 983040 | tf_op jit(solution)/shard_map/psum | solution.py:78
  133.6 3.1 reduce.2
  136.7 6.0 %reshape.181 = f32[2048,8,16]{2,1,0:T(8,128)} reshape(f32[8,32768]{1,0:T(8,128)S(1)} %reduce.2) | data formatting | bytes 2097152
  142.7 5.4 %copy.112 = f32[16,8,8,256]{3,2,1,0:T(8,128)S(1)} copy(f32[16,8,8,256]{0,2,3,1:T(8,128)} %bitcast.173) | data formatting | bytes 2097152 | tf_op jit(solution)/shard_map/all_to_all | solution.py:43
  149.7 130.9 %while.15 = (s32[]{:T(128)}, f32[16,16384]{1,0:T(8,128)S(1)}, f32[16,16384]{1,0:T(8,128)S(1)}, f32[16,16384]{1,0:T(8,128)}, f32[16,16384]{1,0:T(8,128)}, /*index...) while((s32[]{:T(128)}, f32[16,16384]{1,0:T(8,128)S(1)}, ...), condition=%wide.region_4.5_spmd.clone, body=%wide.region_2.4_spmd.clone.sunk | while | flops 1835075 | bytes 18522676 | solution.py:115
  151.6 1.3 constant_dynamic-slice_fusion.14
  156.2 1.9 dynamic_update_slice.46
  159.8 1.3 constant_dynamic-slice_fusion.14
  164.3 1.9 dynamic_update_slice.46
  167.9 1.3 constant_dynamic-slice_fusion.14
  172.5 1.9 dynamic_update_slice.46
  176.1 1.3 constant_dynamic-slice_fusion.14
  180.7 1.9 dynamic_update_slice.46
  184.2 1.3 constant_dynamic-slice_fusion.14
  188.8 1.9 dynamic_update_slice.46
  192.4 1.3 constant_dynamic-slice_fusion.14
  197.0 1.9 dynamic_update_slice.46
  200.6 1.3 constant_dynamic-slice_fusion.14
  205.1 1.9 dynamic_update_slice.46
  208.7 1.3 constant_dynamic-slice_fusion.14
  213.3 1.9 dynamic_update_slice.46
  216.9 1.3 constant_dynamic-slice_fusion.14
  221.4 2.0 dynamic_update_slice.46
  225.0 1.3 constant_dynamic-slice_fusion.14
  229.6 2.0 dynamic_update_slice.46
  233.2 1.3 constant_dynamic-slice_fusion.14
  237.8 2.0 dynamic_update_slice.46
  241.4 1.3 constant_dynamic-slice_fusion.14
  246.0 2.0 dynamic_update_slice.46
  249.6 1.3 constant_dynamic-slice_fusion.14
  254.1 2.0 dynamic_update_slice.46
  257.8 1.3 constant_dynamic-slice_fusion.14
  262.3 2.0 dynamic_update_slice.46
  265.9 1.3 constant_dynamic-slice_fusion.14
  270.5 2.0 dynamic_update_slice.46
  278.7 2.0 dynamic_update_slice.46
  280.6 1.5 copy.157
  282.2 1.5 fusion.16
  284.8 3.5 %all-to-all-start.2 = ((bf16[16,64,256]{2,0,1:T(8,128)(2,1)}), bf16[16,64,256]{2,0,1:T(8,128)(2,1)S(1)}, u32[]{:S(2)}, u32[]{:S(2)}) async-start(bf16[16,64,256]{2,0,1:T(8,128)(2,1)} %copy.130), calls=%async_computation.2 | async-start | bytes 1048576 | tf_op jit(solution)/shard_map/all_to_all | solution.py:120
  289.4 11.5 %all-to-all-done.2 = bf16[16,64,256]{2,0,1:T(8,128)(2,1)S(1)} async-done(((bf16[16,64,256]{2,0,1:T(8,128)(2,1)}), bf16[16,64,256]{2,0,1:T(8,128)(2,1)S(1)}, u32[]{:S(2)}, u32[]{:S(2)}) %all-to-all-start.2) | async-done | bytes 524320 | tf_op jit(solution)/shard_map/all_to_all | solution.py:120
  300.9 8.9 %all-to-all-start.3 = ((f32[16,64,256]{2,0,1:T(8,128)}), f32[16,64,256]{2,0,1:T(8,128)S(1)}, u32[]{:S(2)}, u32[]{:S(2)}) async-start(f32[16,64,256]{2,0,1:T(8,128)} %bitcast.132), calls=%async_computation.3 | async-start | bytes 2097152 | tf_op jit(solution)/shard_map/all_to_all | solution.py:127
  310.2 3.0 fusion.2
  314.1 12.1 %all-to-all-done.3 = f32[16,64,256]{2,0,1:T(8,128)S(1)} async-done(((f32[16,64,256]{2,0,1:T(8,128)}), f32[16,64,256]{2,0,1:T(8,128)S(1)}, u32[]{:S(2)}, u32[]{:S(2)}) %all-to-all-start.3) | async-done | bytes 1048608 | tf_op jit(solution)/shard_map/all_to_all | solution.py:127
  326.8 1.6 copy.135
  (306 shorter events, 84.0 us)
Async XLA Ops:
  0.6 83.6 %copy-start = (bf16[256,160]{0,1:T(8,128)(2,1)S(1)}, bf16[256,160]{0,1:T(8,128)(2,1)}, u32[]{:S(2)}) copy-start(bf16[256,160]{0,1:T(8,128)(2,1)} %param.24) | copy-start | bytes 245764
  2.0 14.3 %copy-start.4 = (bf16[8,3,2048]{2,0,1:T(8,128)(2,1)S(1)}, bf16[8,3,2048]{2,0,1:T(8,128)(2,1)}, u32[]{:S(2)}) copy-start(bf16[8,3,2048]{2,0,1:T(8,128)(2,1)} %param.31) | copy-start | bytes 294916
  7.1 45.2 %collective-permute-start = (bf16[2,16,8,256]{3,2,1,0:T(8,128)(2,1)S(1)}, bf16[2,16,8,256]{3,2,1,0:T(8,128)(2,1)S(1)}, u32[]{:S(2)}, u32[]{:S(2)}) collective-permute-start(bf16[2,16,8,256]{3,2,1,0:T(8,128)(2,1)S(1)} %bitcast.199), channel_id=1, source_target_pairs={{0,4},{4,0},{8,12},{12,8},{16,20},{20,16},{24,28},{28,24},{1,5},{5... | collective-permute-start | bytes 393224 | tf_op jit(solution)/shard_map/ppermute | solution.py:60
  10.2 46.1 %collective-permute-start.1 = (bf16[2,16,8,256]{3,2,1,0:T(8,128)(2,1)S(1)}, bf16[2,16,8,256]{3,2,1,0:T(8,128)(2,1)S(1)}, u32[]{:S(2)}, u32[]{:S(2)}) collective-permute-start(bf16[2,16,8,256]{3,2,1,0:T(8,128)(2,1)S(1)} %bitcast.198), channel_id=1, source_target_pairs={{0,8},{4,12},{8,0},{12,4},{16,24},{20,28},{24,16},{28,20},{1,9},{5... | collective-permute-start | bytes 393224 | tf_op jit(solution)/shard_map/ppermute | solution.py:60
  11.8 46.0 %collective-permute-start.2 = (bf16[2,16,8,256]{3,2,1,0:T(8,128)(2,1)S(1)}, bf16[2,16,8,256]{3,2,1,0:T(8,128)(2,1)S(1)}, u32[]{:S(2)}, u32[]{:S(2)}) collective-permute-start(bf16[2,16,8,256]{3,2,1,0:T(8,128)(2,1)S(1)} %bitcast.197), channel_id=1, source_target_pairs={{0,12},{4,8},{8,4},{12,0},{16,28},{20,24},{24,20},{28,16},{1,13},{... | collective-permute-start | bytes 393224 | tf_op jit(solution)/shard_map/ppermute | solution.py:60
  11.9 45.9 %collective-permute-start.3 = (bf16[2,16,8,256]{3,2,1,0:T(8,128)(2,1)S(1)}, bf16[2,16,8,256]{3,2,1,0:T(8,128)(2,1)S(1)}, u32[]{:S(2)}, u32[]{:S(2)}) collective-permute-start(bf16[2,16,8,256]{3,2,1,0:T(8,128)(2,1)S(1)} %bitcast.196), channel_id=1, source_target_pairs={{0,16},{4,20},{8,24},{12,28},{16,0},{20,4},{24,8},{28,12},{1,17},{... | collective-permute-start | bytes 393224 | tf_op jit(solution)/shard_map/ppermute | solution.py:60
  15.0 42.9 %collective-permute-start.4 = (bf16[2,16,8,256]{3,2,1,0:T(8,128)(2,1)S(1)}, bf16[2,16,8,256]{3,2,1,0:T(8,128)(2,1)S(1)}, u32[]{:S(2)}, u32[]{:S(2)}) collective-permute-start(bf16[2,16,8,256]{3,2,1,0:T(8,128)(2,1)S(1)} %bitcast.195), channel_id=1, source_target_pairs={{0,20},{4,16},{8,28},{12,24},{16,4},{20,0},{24,12},{28,8},{1,21},{... | collective-permute-start | bytes 393224 | tf_op jit(solution)/shard_map/ppermute | solution.py:60
  22.9 10.1 %copy-start.3 = (f32[8,16,2048]{2,1,0:T(8,128)S(1)}, f32[8,16,2048]{2,1,0:T(8,128)}, u32[]{:S(2)}) copy-start(f32[8,16,2048]{2,1,0:T(8,128)} %param.30) | copy-start | bytes 3145732
  28.1 37.2 %all-to-all-start.1 = ((f32[8,1,6144]{2,1,0:T(1,128)}), f32[8,1,6144]{2,1,0:T(1,128)S(1)}, u32[]{:S(2)}, u32[]{:S(2)}) async-start(f32[8,1,6144]{2,1,0:T(1,128)} %reshape.182), calls=%async_computation.1 | async-start | bytes 393216 | tf_op jit(solution)/shard_map/all_to_all | solution.py:44
  37.7 5.8 %copy-start.9 = (s32[64]{0:T(128)S(1)}, s32[64]{0:T(128)}, u32[]{:S(2)}) copy-start(s32[64]{0:T(128)} %param.33) | copy-start | bytes 772
  37.7 5.9 %copy-start.11 = (s32[64]{0:T(128)S(1)}, s32[64]{0:T(128)}, u32[]{:S(2)}) copy-start(s32[64]{0:T(128)} %param.32) | copy-start | bytes 772
  37.7 5.9 %copy-start.6 = (f32[4,256]{1,0:T(4,128)S(1)}, f32[4,256]{1,0:T(4,128)}, u32[]{:S(2)}) copy-start(f32[4,256]{1,0:T(4,128)} %param.22) | copy-start | bytes 12292
  37.7 5.9 %copy-start.5 = (f32[16,256]{1,0:T(8,128)S(1)}, f32[16,256]{1,0:T(8,128)}, u32[]{:S(2)}) copy-start(f32[16,256]{1,0:T(8,128)} %param.27) | copy-start | bytes 49156
  37.7 6.1 %copy-start.10 = (s32[64]{0:T(128)S(1)}, s32[64]{0:T(128)}, u32[]{:S(2)}) copy-start(s32[64]{0:T(128)} %param.35) | copy-start | bytes 772
  52.3 6.9 %collective-permute-start.5 = (bf16[2,16,8,256]{3,2,1,0:T(8,128)(2,1)S(1)}, bf16[2,16,8,256]{3,2,1,0:T(8,128)(2,1)S(1)}, u32[]{:S(2)}, u32[]{:S(2)}) collective-permute-start(bf16[2,16,8,256]{3,2,1,0:T(8,128)(2,1)S(1)} %bitcast.201), channel_id=1, source_target_pairs={{0,24},{4,28},{8,16},{12,20},{16,8},{20,12},{24,0},{28,4},{1,25},{... | collective-permute-start | bytes 393224 | tf_op jit(solution)/shard_map/ppermute | solution.py:60
  56.2 7.8 %collective-permute-start.6 = (bf16[2,16,8,256]{3,2,1,0:T(8,128)(2,1)S(1)}, bf16[2,16,8,256]{3,2,1,0:T(8,128)(2,1)S(1)}, u32[]{:S(2)}, u32[]{:S(2)}) collective-permute-start(bf16[2,16,8,256]{3,2,1,0:T(8,128)(2,1)S(1)} %bitcast.200), channel_id=1, source_target_pairs={{0,28},{4,24},{8,20},{12,16},{16,12},{20,8},{24,4},{28,0},{1,29},{... | collective-permute-start | bytes 393224 | tf_op jit(solution)/shard_map/ppermute | solution.py:60
  64.1 12.7 %copy-start.2 = (bf16[2,16,64,256]{3,2,1,0:T(8,128)(2,1)}, bf16[2,16,64,256]{3,2,1,0:T(8,128)(2,1)S(1)}, u32[]{:S(2)}) copy-start(bf16[2,16,64,256]{3,2,1,0:T(8,128)(2,1)S(1)} %constant_dynamic-update-slice_fusion) | copy-start | bytes 3145732
  65.3 68.2 %all-to-all-start = ((f32[8,1,32768]{2,1,0:T(1,128)}), f32[8,1,32768]{2,1,0:T(1,128)S(1)}, u32[]{:S(2)}, u32[]{:S(2)}) async-start(f32[8,1,32768]{2,1,0:T(1,128)} %reshape.180), calls=%async_computation | async-start | bytes 2097152 | tf_op jit(solution)/shard_map/all_to_all | solution.py:43
  72.1 9.2 %copy-start.7 = (f32[256]{0:T(256)S(1)}, f32[256]{0:T(256)}, u32[]{:S(2)}) copy-start(f32[256]{0:T(256)} %param.23) | copy-start | bytes 3076
  76.8 53.4 %copy-start.12 = (bf16[128,256]{1,0:T(8,128)(2,1)S(1)}, bf16[128,256]{1,0:T(8,128)(2,1)}, u32[]{:S(2)}) copy-start(bf16[128,256]{1,0:T(8,128)(2,1)} %param.25) | copy-start | bytes 196612
  76.8 53.4 %copy-start.13 = (f32[256]{0:T(256)S(1)}, f32[256]{0:T(256)}, u32[]{:S(2)}) copy-start(f32[256]{0:T(256)} %param.26) | copy-start | bytes 3076
  148.7 1.0 copy-start.14
  149.7 132.5 %copy-start.8 = (f32[256]{0:T(256)S(1)}, f32[256]{0:T(256)}, u32[]{:S(2)}) copy-start(f32[256]{0:T(256)} %param.28) | copy-start | bytes 3076
  284.8 16.1 %all-to-all-start.2 = ((bf16[16,64,256]{2,0,1:T(8,128)(2,1)}), bf16[16,64,256]{2,0,1:T(8,128)(2,1)S(1)}, u32[]{:S(2)}, u32[]{:S(2)}) async-start(bf16[16,64,256]{2,0,1:T(8,128)(2,1)} %copy.130), calls=%async_computation.2 | async-start | bytes 1048576 | tf_op jit(solution)/shard_map/all_to_all | solution.py:120
  300.9 25.3 %all-to-all-start.3 = ((f32[16,64,256]{2,0,1:T(8,128)}), f32[16,64,256]{2,0,1:T(8,128)S(1)}, u32[]{:S(2)}, u32[]{:S(2)}) async-start(f32[16,64,256]{2,0,1:T(8,128)} %bitcast.132), calls=%async_computation.3 | async-start | bytes 2097152 | tf_op jit(solution)/shard_map/all_to_all | solution.py:127
  310.2 18.2 %copy-start.1 = (bf16[256,160]{0,1:T(8,128)(2,1)S(1)}, bf16[256,160]{0,1:T(8,128)(2,1)}, u32[]{:S(2)}) copy-start(bf16[256,160]{0,1:T(8,128)(2,1)} %param.24) | copy-start | bytes 245764
